TPU v7x, 256 devices: a whole 4x4x8 slice. The times are simulated.
256 devices in a mesh: replica: 32 (over x, z_lo, y), fsdp: 8 (over z_hi, core).
Axes of the slice: x: 4, y: 4, z: 8 (z_hi: 4, z_lo: 2; z = z_hi * 2 + z_lo), core: 2. Of those that a mesh axis runs over, the one named last changes fastest.
Arguments:
- tokens: bfloat16 [131072, 4096], P(('replica', 'fsdp')), may hold values from -6 to 6
- key_cotangent: bfloat16 [131072, 512], P(('replica', 'fsdp')), may hold values from -0.1875 to 0.1875
- key_weight: bfloat16 [131072, 512], P(('replica', 'fsdp')), may hold values from -0.09375 to 0.09375
- first_moment: float32 [131072, 512], P(('replica', 'fsdp')), may hold values from -6 to 6
- second_moment: float32 [131072, 512], P(('replica', 'fsdp')), may hold values from 0.1 to 3
- local_slab: bfloat16 [49152, 4096], P(('replica', 'fsdp')), as said below
- outer_params: float32 [1536, 4096], P('fsdp', 'replica')
- outer_momentum: float32 [1536, 4096], P('fsdp', 'replica'), may hold values from -3 to 3
Outputs:
- projected: bfloat16 [131072, 512], P(('replica', 'fsdp'))
- new_weight: bfloat16 [131072, 512], P(('replica', 'fsdp'))
- new_first: float32 [131072, 512], P(('replica', 'fsdp'))
- new_second: float32 [131072, 512], P(('replica', 'fsdp'))
- new_outer: float32 [1536, 4096], P('fsdp', 'replica')
- new_momentum: float32 [1536, 4096], P('fsdp', 'replica')
- new_local: bfloat16 [49152, 4096], P(('replica', 'fsdp'))
Inputs may be any that keep to these rules, and one draw needn't show every extreme that they name: `local_slab`: each replica's fragment equals outer_params plus a drift that the replicas partly share.
All inputs are finite; a program needn't handle non-finite values.
Results may differ from a plain program's by a relative error of at most 0.00045.
Values may be sent and summed in bfloat16 or wider, within the bound.
A program may use at most 128 MiB of HBM per device.

v0:
```python
import jax
import jax.numpy as jnp
from jax import lax
from jax.sharding import PartitionSpec as P

BETA_ONE = 0.9
BETA_TWO = 0.95
INNER_RATE = 0.001
DECAY_RATE = 0.1
EPSILON = 1e-08
FIRST_FIX = 1.0 - (0.9**50) ** 2
SECOND_FIX = 1.0 - (0.95**50) ** 2
OUTER_RATE = 0.7
OUTER_MOMENTUM = 0.9
MERGE_WEIGHT = 0.5


def outer_update(outer_params, outer_momentum, summed, replicas):
    average = summed / replicas
    pseudo_grad = outer_params - average
    new_momentum = OUTER_MOMENTUM * outer_momentum + pseudo_grad
    new_outer = outer_params - OUTER_RATE * (pseudo_grad + OUTER_MOMENTUM * new_momentum)
    return (new_outer, new_momentum)


def shards(
    tokens,
    key_cotangent,
    key_weight,
    first_moment,
    second_moment,
    local_slab,
    outer_params,
    outer_momentum,
):
    columns = tokens
    projected = jnp.dot(
        columns,
        lax.all_gather(key_weight, "fsdp", axis=0, tiled=True),
        preferred_element_type=jnp.float32,
    ).astype(jnp.bfloat16)
    columns = tokens
    gradient = lax.psum_scatter(
        lax.dot_general(
            columns, key_cotangent, (((0,), (0,)), ((), ())), preferred_element_type=jnp.float32
        ),
        "fsdp",
        scatter_dimension=0,
        tiled=True,
    )
    new_first = BETA_ONE * first_moment + (1.0 - BETA_ONE) * gradient
    new_second = BETA_TWO * second_moment + (1.0 - BETA_TWO) * gradient * gradient
    weight_f = key_weight.astype(jnp.float32)
    update = (
        new_first / FIRST_FIX / (jnp.sqrt(new_second / SECOND_FIX) + EPSILON)
        + DECAY_RATE * weight_f
    )
    new_weight = (weight_f - INNER_RATE * update).astype(jnp.bfloat16)
    replicas = lax.axis_size("replica")
    column_count = outer_params.shape[1]
    slab_f = local_slab.astype(jnp.float32)
    whole_params, whole_momentum = (
        lax.all_gather(outer_params, "replica", axis=1, tiled=True),
        lax.all_gather(outer_momentum, "replica", axis=1, tiled=True),
    )
    summed = lax.psum(slab_f, "replica")
    whole_outer, whole_new_momentum = outer_update(whole_params, whole_momentum, summed, replicas)
    first_column = lax.axis_index("replica") * column_count
    new_outer = lax.dynamic_slice_in_dim(whole_outer, first_column, column_count, 1)
    new_momentum = lax.dynamic_slice_in_dim(whole_new_momentum, first_column, column_count, 1)
    new_local = (MERGE_WEIGHT * slab_f + (1.0 - MERGE_WEIGHT) * whole_outer).astype(jnp.bfloat16)
    return (projected, new_weight, new_first, new_second, new_outer, new_momentum, new_local)


def solution(mesh):
    return jax.shard_map(
        shards,
        mesh=mesh,
        in_specs=(
            P(("replica", "fsdp"), None),
            P(("replica", "fsdp"), None),
            P(("replica", "fsdp"), None),
            P(("replica", "fsdp"), None),
            P(("replica", "fsdp"), None),
            P(("replica", "fsdp"), None),
            P("fsdp", "replica"),
            P("fsdp", "replica"),
        ),
        out_specs=(
            P(("replica", "fsdp"), None),
            P(("replica", "fsdp"), None),
            P(("replica", "fsdp"), None),
            P(("replica", "fsdp"), None),
            P("fsdp", "replica"),
            P("fsdp", "replica"),
            P(("replica", "fsdp"), None),
        ),
        check_vma=False,
    )
```

profile of v0, /device:TPU:1, one launch (start us, length us, event | category | flops | bytes accessed | tf_op | source)
XLA Modules:
  0.0 469.1 jit_solution(1939503694912655858)
XLA Ops:
  7.2 0.0 copy-start
  7.2 0.0 all-gather.6.cloned.1.call-start
  7.2 0.7 all-gather.6.cloned.1.call-update
  7.9 0.0 all-gather.8.cloned.1.call-start
  8.0 0.7 all-gather.8.cloned.1.call-update
  8.7 0.0 all-gather.4.cloned.1.call-start
  8.7 0.7 all-gather.4.cloned.1.call-update
  9.4 0.0 reduce-scatter.2.cloned.1.call-start
  9.4 0.0 copy-done
  9.5 7.8 %fusion.5 = f32[4096,512]{1,0:T(8,128)} fusion(bf16[512,4096]{1,0:T(8,128)(2,1)} %param.8, bf16[512,512]{1,0:T(8,128)(2,1)S(1)} %copy-done), kind=kOutput, calls=%fused_computation.15 | convolution fusion | flops 2147483648 | bytes 13107200 | tf_op jit(solution)/shard_map/dot_general | solution.py:44
  17.3 0.0 copy-start.1
  17.3 0.0 reduce-scatter.2.cloned.1.call-update
  17.3 1.4 copy-done.1
  18.7 177.2 %all-reduce.1 = f32[192,4096]{1,0:T(8,128)} all-reduce(bf16[192,4096]{1,0:T(8,128)(2,1)S(1)} %copy-done.1), channel_id=1, replica_groups=mesh['replica'=32,'fsdp'=8] {'replica'}, use_global_device_ids=true, to_apply=%region_1.0 | all-reduce | flops 786432 | bytes 4718592 | tf_op jit(solution)/shard_map/psum | solution.py:66
  195.9 0.0 all-gather.6.cloned.1.call-done
  195.9 91.4 %all-gather.8.cloned.1.call-done = f32[192,4096]{1,0:T(8,128)} async-done(((f32[192,128]{1,0:T(8,128)}), f32[192,4096]{1,0:T(8,128)}) %all-gather.8.cloned.1.call-update) | async-done | bytes 3145744 | tf_op jit(solution)/shard_map/all_gather | solution.py:64
  287.3 6.2 %multiply_convert_fusion = (bf16[192,4096]{1,0:T(8,128)(2,1)}, f32[192,4096]{1,0:T(8,128)S(1)}, f32[192,4096]{1,0:T(8,128)S(1)}) fusion(bf16[192,4096]{1,0:T(8,128)(2,1)S(1)} %copy-done.1, f32[192,4096]{1,0:T(8,128)} %all-gather.6.cloned.1.call-done, f32[192,4096]{1,0:T(8,128)} %all-gather.8.cloned.1.call-done, f32[192,4096]{1,0:T(8,128)} %all-reduce.1), kind=kLoop, calls=%fused_computation | loop fusion | flops 9437184 | bytes 18874368 | tf_op jit(solution)/shard_map/convert_element_type | solution.py:71
  293.4 0.7 constant_dynamic-slice_fusion
  294.1 0.0 copy-start.2
  294.1 0.0 copy-start.3
  294.1 0.0 copy-start.4
  294.1 66.1 %all-gather.4.cloned.1.call-done = bf16[4096,512]{1,0:T(8,128)(2,1)} async-done(((bf16[512,512]{1,0:T(8,128)(2,1)}), bf16[4096,512]{1,0:T(8,128)(2,1)}) %all-gather.4.cloned.1.call-update) | async-done | bytes 4194320 | tf_op jit(solution)/shard_map/all_gather | solution.py:39
  360.2 6.6 %convolution_convert_fusion = bf16[512,512]{1,0:T(8,128)(2,1)} fusion(bf16[512,4096]{1,0:T(8,128)(2,1)} %param.8, bf16[4096,512]{1,0:T(8,128)(2,1)} %all-gather.4.cloned.1.call-done), kind=kOutput, calls=%fused_computation.7 | convolution fusion | flops 2147745792 | bytes 8912896 | tf_op jit(solution)/shard_map/dot_general | solution.py:37
  366.8 92.3 %reduce-scatter.2.cloned.1.call-done = f32[512,512]{1,0:T(8,128)} async-done(((f32[4096,512]{1,0:T(8,128)}), f32[512,512]{1,0:T(8,128)}) %reduce-scatter.2.cloned.1.call-update) | async-done | bytes 1048592 | tf_op jit(solution)/shard_map/reduce_scatter | solution.py:43
  459.1 0.0 copy-done.2
  459.1 0.0 copy-done.3
  459.1 0.0 copy-done.4
  459.1 3.4 fusion.2
Async XLA Ops:
  7.2 2.3 copy-start
  7.2 188.7 %all-gather.6.cloned.1.call-start = ((), (), s32[]{:S(2)}) async-start(), calls=%async_computation.3 | async-start | bytes 3244032 | tf_op jit(solution)/shard_map/all_gather | solution.py:63
  7.9 279.3 %all-gather.8.cloned.1.call-start = ((), (), s32[]{:S(2)}) async-start(), calls=%async_computation.4 | async-start | bytes 3244032 | tf_op jit(solution)/shard_map/all_gather | solution.py:64
  8.7 351.6 %all-gather.4.cloned.1.call-start = ((), (), s32[]{:S(2)}) async-start(), calls=%async_computation.1 | async-start | bytes 4718592 | tf_op jit(solution)/shard_map/all_gather | solution.py:39
  9.4 449.7 %reduce-scatter.2.cloned.1.call-start = ((), (), s32[]{:S(2)}) async-start(), calls=%async_computation.2 | async-start | bytes 9437184 | tf_op jit(solution)/shard_map/reduce_scatter | solution.py:43
  17.3 1.4 copy-start.1
  294.1 165.0 %copy-start.2 = (bf16[512,512]{1,0:T(8,128)(2,1)S(1)}, bf16[512,512]{1,0:T(8,128)(2,1)}, u32[]{:S(2)}) copy-start(bf16[512,512]{1,0:T(8,128)(2,1)} %param.10) | copy-start | bytes 1572868
  294.1 165.0 %copy-start.3 = (f32[512,512]{1,0:T(8,128)S(1)}, f32[512,512]{1,0:T(8,128)}, u32[]{:S(2)}) copy-start(f32[512,512]{1,0:T(8,128)} %param.11) | copy-start | bytes 3145732
  294.1 165.0 %copy-start.4 = (f32[512,512]{1,0:T(8,128)S(1)}, f32[512,512]{1,0:T(8,128)}, u32[]{:S(2)}) copy-start(f32[512,512]{1,0:T(8,128)} %param.12) | copy-start | bytes 3145732
Sparse Core Ops, SparseCore 0:
  9.7 138.1 all-gather.5
  149.6 137.5 all-gather.7
  289.1 71.0 all-gather.3
  362.6 96.4 reduce-scatter.1
where the time goes:
time: 471 us; the launch traced here: 469 us
  waiting for transfers between devices  252 us (54%)
  blocking collectives  177 us (38%)
  matrix products  14.4 us (3%)
  between operations  13.8 us (3%)
  other arithmetic  9.56 us (2%)
    psum x1, blocking collectives, shards(): summed = lax.psum(slab_f, 'replica')  177 us
    reduce_scatter x1, waiting for transfers between devices, shards(): lax.psum_scatter(lax.dot_general(columns, key_cotangent, (((0,), (0,)), (...  92.3 us
    all_gather x1, waiting for transfers between devices, shards(): lax.all_gather(outer_momentum, 'replica', axis=1, tiled=True)  91.4 us
    all_gather x1, waiting for transfers between devices, shards(): lax.all_gather(key_weight, 'fsdp', axis=0, tiled=True)  66.1 us
  transfers between devices with their start and end apart: 4, of which 3 were waited for; matrix products, arithmetic and copies ran while one was open for 5% of the time, Pallas kernels for 0%

commit v1 on v0

v1 whole, which is shorter than its diff:
```python
import jax
import jax.numpy as jnp
from jax import lax
from jax.experimental import pallas as pl
from jax.experimental.pallas import tpu as pltpu
from jax.sharding import PartitionSpec as P

BETA_ONE = 0.9
BETA_TWO = 0.95
INNER_RATE = 0.001
DECAY_RATE = 0.1
EPSILON = 1e-08
FIRST_FIX = 1.0 - (0.9**50) ** 2
SECOND_FIX = 1.0 - (0.95**50) ** 2
OUTER_RATE = 0.7
OUTER_MOMENTUM = 0.9
MERGE_WEIGHT = 0.5

MESH = pl.DeviceIdType.MESH
F32, BF16 = jnp.float32, jnp.bfloat16
B = 512
HB = 256
ROWS = 192
HR = 96
LANES = 128
REPLICAS = 32

W_UP, W_DOWN, W_CORE, W_UP2, W_DOWN2, W_CORE_UP, W_CORE_DOWN, W_CORE_FAR = range(8)
X_CORE = 8
C_CORE = 12
G_UP1, G_DOWN1, G_UP, G_DOWN, G_UP2, G_DOWN2 = range(13, 19)
RS_A0, RS_A1, RS_B0, RS_B1 = 19, 22, 25, 28
RS_Z = 31
AG_Z = 32
AG_A0, AG_A1, AG_B0, AG_B1 = 33, 36, 39, 42
W_CORE_FAR2 = 45
N_REMOTE = 46


def kernel(
    tok_ref, cot_ref, w_ref, first_ref, second_ref, slab_ref, outer_ref, mom_ref,
    proj_out, neww_out, first_out, second_out, outer_out, mom_out, local_out,
    xb, xo, cb, co, wb, g, r1, ru, ra, m1, m2,
    slab, ra0, ra1, pa0, pa1, rb0, rb1, tb, rz, po, pm, agb, nl,
    acc, pj, nw,
    ss, rs, ls, xs, slab_s, os,
):
    r = lax.axis_index("replica")
    f = lax.axis_index("fsdp")
    x, zl, y = lax.div(r, 8), lax.rem(lax.div(r, 4), 2), lax.rem(r, 4)
    zh, c = lax.div(f, 2), lax.rem(f, 2)

    def turn(value, step, size=4):
        return lax.rem(value + step + size, size)

    def dev(x_, zl_, y_, zh_, c_):
        return {"replica": (x_ * 2 + zl_) * 4 + y_, "fsdp": zh_ * 2 + c_}

    def at_x(d):
        return dev(turn(x, d), zl, y, zh, c)

    def at_y(d):
        return dev(x, zl, turn(y, d), zh, c)

    up, down = dev(x, zl, y, turn(zh, 1), c), dev(x, zl, y, turn(zh, -1), c)
    pair = dev(x, 1 - zl, y, zh, c)
    core = dev(x, zl, y, zh, 1 - c)

    def remote(place, src, dst, device):
        return pltpu.make_async_remote_copy(
            src_ref=src, dst_ref=dst, send_sem=ss.at[place], recv_sem=rs.at[place],
            device_id=device, device_id_type=MESH,
        )

    sent = []

    def send(place, src, dst, device):
        copy = remote(place, src, dst, device)
        copy.start()
        sent.append(copy)
        return copy

    def rows(total, step, body):
        def one(i, _):
            body(pl.ds(pl.multiple_of(i * step, step), step))
            return 0
        lax.fori_loop(0, total // step, one, 0)

    own_w = pltpu.make_async_copy(w_ref, wb.at[f], ls.at[0])
    own_w.start()
    own_c = pltpu.make_async_copy(cot_ref, cb, ls.at[1])
    own_c.start()
    own_x = []
    for k in range(8):
        copy = pltpu.make_async_copy(tok_ref.at[:, k * B:(k + 1) * B], xb.at[k], xs.at[k])
        copy.start()
        own_x.append(copy)

    def slab_copy(k):
        return pltpu.make_async_copy(
            slab_ref.at[:, k * LANES:(k + 1) * LANES], slab.at[k // 4, k % 4], slab_s.at[k]
        )
    for k in range(32):
        slab_copy(k).start()
    own_m1 = pltpu.make_async_copy(first_ref, m1, ls.at[2])
    own_m2 = pltpu.make_async_copy(second_ref, m2, ls.at[3])
    own_po = pltpu.make_async_copy(outer_ref, po, ls.at[4])
    own_pm = pltpu.make_async_copy(mom_ref, pm, ls.at[5])
    for copy in (own_po, own_pm, own_m1, own_m2):
        copy.start()

    barrier = pltpu.get_barrier_semaphore()
    partners = [up, down, core, pair] + [at_x(d) for d in (1, 2, 3)] + [at_y(d) for d in (1, 2, 3)]
    for partner in partners:
        pl.semaphore_signal(barrier, inc=1, device_id=partner, device_id_type=MESH)
    pl.semaphore_wait(barrier, len(partners))

    own_w.wait()
    w_up = send(W_UP, wb.at[f], wb.at[f], up)
    w_down = send(W_DOWN, wb.at[f], wb.at[f], down)
    w_core = send(W_CORE, wb.at[f], wb.at[f], core)

    own_c.wait()
    c_core = send(C_CORE, cb, co, core)
    for copy in own_x:
        copy.wait()
    x_core = {}
    for d in (2, 1, 3, 0):
        x_core[d] = send(X_CORE + d, xb.at[2 * turn(zh, d) + 1 - c], xo.at[d], core)

    for k in range(32):
        slab_copy(k).wait()
    a0, a1 = [], []
    for d in (1, 2, 3):
        a0.append(send(RS_A0 + d - 1, slab.at[pl.ds(2 * turn(x, d), 2), :, 0:HR], ra0.at[d - 1], at_x(d)))
        a1.append(send(RS_A1 + d - 1, slab.at[:, turn(y, d), HR:ROWS], ra1.at[d - 1], at_y(d)))

    def gradient(d):
        x_core[d].wait_recv()
        dims = (((0,), (0,)), ((), ()))
        mine = lax.dot_general(xb[2 * turn(zh, d) + c], cb[...], dims, preferred_element_type=F32)
        g[d] = mine
        other = lax.dot_general(xo[d], co[...], dims, preferred_element_type=F32)
        g[d] += other

    c_core.wait_recv()
    gradient(2)
    g_up1 = send(G_UP1, g.at[2, 0:HB], r1.at[0], up)
    g_down1 = send(G_DOWN1, g.at[2, HB:B], r1.at[1], down)
    gradient(1)
    g_up = send(G_UP, g.at[1, HB:B], ru.at[0], up)
    gradient(3)
    g_down = send(G_DOWN, g.at[3, 0:HB], ru.at[1], down)
    gradient(0)

    def project(k, start=False):
        part = jnp.dot(xb[k], wb[k], preferred_element_type=F32)
        if start:
            acc[...] = part
        else:
            acc[...] += part

    project(f, True)

    for copy in a0:
        copy.wait_recv()
    for kk in range(2):
        for yy in range(4):
            pa0[kk, yy] = (
                slab[2 * x + kk, yy, 0:HR].astype(F32) + ra0[0, kk, yy].astype(F32)
                + ra0[1, kk, yy].astype(F32) + ra0[2, kk, yy].astype(F32)
            )
    b0 = [send(RS_B0 + d - 1, pa0.at[:, turn(y, d)], rb0.at[d - 1], at_y(d)) for d in (1, 2, 3)]
    for copy in a1:
        copy.wait_recv()
    for k in range(8):
        pa1[k] = (
            slab[k, y, HR:ROWS].astype(F32) + ra1[0, k].astype(F32)
            + ra1[1, k].astype(F32) + ra1[2, k].astype(F32)
        )
    b1 = [send(RS_B1 + d - 1, pa1.at[pl.ds(2 * turn(x, d), 2)], rb1.at[d - 1], at_x(d)) for d in (1, 2, 3)]
    for copy in b0:
        copy.wait_recv()
    for copy in b1:
        copy.wait_recv()
    for kk in range(2):
        tb[kk, 0:HR] = pa0[kk, y] + rb0[0, kk] + rb0[1, kk] + rb0[2, kk]
        tb[kk, HR:ROWS] = pa1[2 * x + kk] + rb1[0, kk] + rb1[1, kk] + rb1[2, kk]
    z_sum = send(RS_Z, tb.at[1 - zl], rz, pair)

    w_core.wait_recv()
    project(2 * zh + 1 - c)

    w_up.wait_recv()
    below = 2 * turn(zh, -1) + c
    w_up2 = send(W_UP2, wb.at[below, 0:HB], wb.at[below, 0:HB], up)
    w_core_up = send(W_CORE_UP, wb.at[below], wb.at[below], core)
    w_down.wait_recv()
    above = 2 * turn(zh, 1) + c
    w_down2 = send(W_DOWN2, wb.at[above, HB:B], wb.at[above, HB:B], down)
    w_core_down = send(W_CORE_DOWN, wb.at[above], wb.at[above], core)

    z_sum.wait_recv()
    own_po.wait()
    own_pm.wait()
    average = (tb[zl] + rz[...]) / REPLICAS
    pseudo_grad = po[...] - average
    new_momentum = OUTER_MOMENTUM * pm[...] + pseudo_grad
    new_outer = po[...] - OUTER_RATE * (pseudo_grad + OUTER_MOMENTUM * new_momentum)
    pm[...] = new_momentum
    agb[2 * x + zl, y] = new_outer
    outs = []

    def put(place, src, dst):
        copy = pltpu.make_async_copy(src, dst, os.at[place])
        copy.start()
        outs.append(copy)

    z_gather = send(AG_Z, agb.at[2 * x + zl, y], agb.at[2 * x + zl, y], pair)
    put(0, pm, mom_out)
    put(1, agb.at[2 * x + zl, y], outer_out)

    g_up1.wait_recv()
    g[1, 0:HB] += r1[0]
    g_up2 = send(G_UP2, g.at[1, 0:HB], ra.at[0], up)
    g_down1.wait_recv()
    g[3, HB:B] += r1[1]
    g_down2 = send(G_DOWN2, g.at[3, HB:B], ra.at[1], down)

    z_gather.wait_recv()
    g0 = [send(AG_A0 + d - 1, agb.at[pl.ds(2 * x, 2), y, 0:HR], agb.at[pl.ds(2 * x, 2), y, 0:HR], at_x(d)) for d in (1, 2, 3)]
    g1 = [send(AG_A1 + d - 1, agb.at[pl.ds(2 * x, 2), y, HR:ROWS], agb.at[pl.ds(2 * x, 2), y, HR:ROWS], at_y(d)) for d in (1, 2, 3)]
    w_core_up.wait_recv()
    w_core_down.wait_recv()
    for s in (-1, 1):
        project(2 * turn(zh, s) + c)
        project(2 * turn(zh, s) + 1 - c)
    for copy in g0:
        copy.wait_recv()
    h0 = [send(AG_B0 + d - 1, agb.at[:, y, 0:HR], agb.at[:, y, 0:HR], at_y(d)) for d in (1, 2, 3)]
    for copy in g1:
        copy.wait_recv()
    h1 = [send(AG_B1 + d - 1, agb.at[pl.ds(2 * x, 2), :, HR:ROWS], agb.at[pl.ds(2 * x, 2), :, HR:ROWS], at_x(d)) for d in (1, 2, 3)]

    g_up.wait_recv()
    g[0, HB:B] += ru[0]
    g_down.wait_recv()
    g[0, 0:HB] += ru[1]

    for copy in h0:
        copy.wait_recv()
    for copy in h1:
        copy.wait_recv()
    for k in range(32):
        block = MERGE_WEIGHT * slab[k // 4, k % 4].astype(F32) + (1.0 - MERGE_WEIGHT) * agb[k // 4, k % 4]
        nl[:, k * LANES:(k + 1) * LANES] = block.astype(BF16)
    put(2, nl, local_out)

    far = 2 * turn(zh, 2) + c
    w_up2.wait_recv()
    w_far = send(W_CORE_FAR, wb.at[far, 0:HB], wb.at[far, 0:HB], core)
    w_down2.wait_recv()
    w_far2 = send(W_CORE_FAR2, wb.at[far, HB:B], wb.at[far, HB:B], core)
    project(far)
    w_far.wait_recv()
    w_far2.wait_recv()
    project(2 * turn(zh, 2) + 1 - c)
    pj[...] = acc[...].astype(BF16)
    put(3, pj, proj_out)

    own_m1.wait()
    own_m2.wait()

    def adam(part, half):
        def body(at):
            grad = g[0, at] + ra[half, pl.ds(at.start - half * HB, at.size)]
            new_first = BETA_ONE * m1[at] + (1.0 - BETA_ONE) * grad
            new_second = BETA_TWO * m2[at] + (1.0 - BETA_TWO) * grad * grad
            weight = wb[f, at].astype(F32)
            update = new_first / FIRST_FIX / (jnp.sqrt(new_second / SECOND_FIX) + EPSILON) + DECAY_RATE * weight
            m1[at] = new_first
            m2[at] = new_second
            nw[at] = (weight - INNER_RATE * update).astype(BF16)

        def one(i, _):
            body(pl.ds(pl.multiple_of(half * HB + i * 32, 32), 32))
            return 0
        lax.fori_loop(0, HB // 32, one, 0)

    g_up2.wait_recv()
    adam(g_up2, 0)
    g_down2.wait_recv()
    adam(g_down2, 1)
    put(4, m1, first_out)
    put(5, m2, second_out)
    put(6, nw, neww_out)
    for copy in sent:
        copy.wait_send()
    for copy in outs:
        copy.wait()


def shards(tokens, key_cotangent, key_weight, first_moment, second_moment, local_slab, outer_params, outer_momentum):
    out_shape = (
        jax.ShapeDtypeStruct((B, B), BF16),
        jax.ShapeDtypeStruct((B, B), BF16),
        jax.ShapeDtypeStruct((B, B), F32),
        jax.ShapeDtypeStruct((B, B), F32),
        jax.ShapeDtypeStruct((ROWS, LANES), F32),
        jax.ShapeDtypeStruct((ROWS, LANES), F32),
        jax.ShapeDtypeStruct((ROWS, 4096), BF16),
    )
    vmem = pltpu.VMEM
    return pl.pallas_call(
        kernel,
        out_shape=out_shape,
        in_specs=[pl.BlockSpec(memory_space=pl.ANY)] * 8,
        out_specs=(pl.BlockSpec(memory_space=pl.ANY),) * 7,
        scratch_shapes=[
            vmem((8, B, B), BF16),
            vmem((4, B, B), BF16),
            vmem((B, B), BF16),
            vmem((B, B), BF16),
            vmem((8, B, B), BF16),
            vmem((4, B, B), F32),
            vmem((2, HB, B), F32),
            vmem((2, HB, B), F32),
            vmem((2, HB, B), F32),
            vmem((B, B), F32),
            vmem((B, B), F32),
            vmem((8, 4, ROWS, LANES), BF16),
            vmem((3, 2, 4, HR, LANES), BF16),
            vmem((3, 8, HR, LANES), BF16),
            vmem((2, 4, HR, LANES), F32),
            vmem((8, HR, LANES), F32),
            vmem((3, 2, HR, LANES), F32),
            vmem((3, 2, HR, LANES), F32),
            vmem((2, ROWS, LANES), F32),
            vmem((ROWS, LANES), F32),
            vmem((ROWS, LANES), F32),
            vmem((ROWS, LANES), F32),
            vmem((8, 4, ROWS, LANES), F32),
            vmem((ROWS, 4096), BF16),
            vmem((B, B), F32),
            vmem((B, B), BF16),
            vmem((B, B), BF16),
            pltpu.SemaphoreType.DMA((N_REMOTE,)),
            pltpu.SemaphoreType.DMA((N_REMOTE,)),
            pltpu.SemaphoreType.DMA((6,)),
            pltpu.SemaphoreType.DMA((8,)),
            pltpu.SemaphoreType.DMA((32,)),
            pltpu.SemaphoreType.DMA((7,)),
        ],
        name="window",
        compiler_params=pltpu.CompilerParams(
            collective_id=0, has_side_effects=True, vmem_limit_bytes=48 << 20
        ),
    )(tokens, key_cotangent, key_weight, first_moment, second_moment, local_slab, outer_params, outer_momentum)


def solution(mesh):
    both = P(("replica", "fsdp"), None)
    cut = P("fsdp", "replica")
    return jax.shard_map(
        shards,
        mesh=mesh,
        in_specs=(both, both, both, both, both, both, cut, cut),
        out_specs=(both, both, both, both, cut, cut, both),
        check_vma=False,
    )
```

time: 471 us -> 147 us (0.31)
  waiting for transfers between devices: 252 us -> 0 us
  blocking collectives: 177 us -> 0 us
  Pallas kernels: 0 us -> 135 us
  matrix products: 14.4 us -> 0 us
  between operations: 13.8 us -> 0.66 us
  other arithmetic: 9.56 us -> 0 us
  local copies, waits for them, and re-layouts: 2.1 us -> 11 us
    psum x1 -> x0, blocking collectives: 177 us -> none  [shards(): summed = lax.psum(slab_f, 'replica')]
    all_gather x3 -> x0, waiting for transfers between devices: 157 us -> none  [the longest x1 91.4 us: shards(): lax.all_gather(outer_momentum, 'replica', axis=1, tiled=True)]
    pallas_call x0 -> x1, Pallas kernels: none -> 135 us  [shards(): pl.pallas_call(kernel, out_shape=out_shape, in_specs=[pl.BlockSpec(memory...]
    reduce_scatter x1 -> x0, waiting for transfers between devices: 92.3 us -> none  [shards(): lax.psum_scatter(lax.dot_general(columns, key_cotangent, (((0,), (0,)), (...]
    dot_general x2 -> x0, matrix products: 14.4 us -> none  [the longest x1 7.8 us: shards(): lax.dot_general(columns, key_cotangent, (((0,), (0,)), ((), ())), preferr...]
    unnamed x10 -> x19, local copies, waits for them, and re-layouts: 1.4 us -> 11 us
    convert_element_type x2 -> x0, other arithmetic: 9.56 us -> none  [the longest x1 6.17 us: shards(): (MERGE_WEIGHT * slab_f + (1.0 - MERGE_WEIGHT) * whole_outer).astype(jnp.b...]
  transfers between devices with their start and end apart: 4 -> 0, of which waited for: 3 -> 0; matrix products, arithmetic and copies ran while one was open for 5% -> 0% of each run, Pallas kernels for 0% -> 0%
where the time goes in v1:
time: 147 us
  Pallas kernels  135 us (92%)
  local copies, waits for them, and re-layouts  11 us (7%)
    pallas_call x1, Pallas kernels, shards(): pl.pallas_call(kernel, out_shape=out_shape, in_specs=[pl.BlockSpec(memory...  135 us
    unnamed x19, local copies, waits for them, and re-layouts  11 us

profile of v1, /device:TPU:1, one launch (start us, length us, event | category | flops | bytes accessed | tf_op | source)
XLA Modules:
  0.0 146.8 jit_solution(9766449083481746646)
XLA Ops:
  0.6 0.0 copy-start
  0.6 1.2 copy-done
  1.9 0.0 copy-start.1
  1.9 1.0 copy-done.1
  2.9 0.0 copy-start.2
  2.9 1.0 copy-done.2
  3.9 0.0 copy-start.3
  3.9 0.9 copy-done.3
  4.8 0.0 copy-start.4
  4.8 0.9 copy-done.4
  5.7 135.1 %window.1 = (bf16[512,512]{1,0:T(8,128)(2,1)S(1)}, bf16[512,512]{1,0:T(8,128)(2,1)S(1)}, f32[512,512]{1,0:T(8,128)S(1)}, f32[512,512]{1,0:T(8,128)S(1)}, f32[192...) custom-call(bf16[512,4096]{1,0:T(8,128)(2,1)} %tok_ref.1, bf16[512,512]{1,0:T(8,128)(2,1)S(1)} %copy-done.1, ...), custom_call_target="tpu_custom_call" | custom-call | tf_op jit(solution)/shard_map/window/pallas_call | solution.py:314
  140.8 0.8 copy.22
  141.6 0.8 copy.23
  142.4 1.0 copy.24
  143.4 0.0 copy-start.5
  143.4 1.0 copy.25
  144.4 0.6 copy.26
  145.0 0.6 copy.27
  145.7 0.0 copy-done.5
  145.7 1.1 copy.28
Async XLA Ops:
  0.6 1.2 copy-start
  1.9 1.0 copy-start.1
  2.9 1.0 copy-start.2
  3.9 0.9 copy-start.3
  4.8 0.9 copy-start.4
  143.4 2.3 %copy-start.5 = (bf16[192,4096]{1,0:T(8,128)(2,1)S(1)}, bf16[192,4096]{1,0:T(8,128)(2,1)}, u32[]{:S(2)}) copy-start(bf16[192,4096]{1,0:T(8,128)(2,1)} %get-tuple-element.20) | copy-start | bytes 4718596

commit v2 on v1

--- a/solution.py
+++ b/solution.py
@@ -37,13 +37,26 @@
 N_REMOTE = 46
 
 
+def packed(v):
+    t = 8.0 * v
+    t2 = t * t
+    t4 = t2 * t2
+    t8 = t4 * t4
+    return jnp.where(v < 0.0, -t8, t8).astype(BF16)
+
+
+def unpacked(p):
+    p = p.astype(F32)
+    v = 0.125 * jnp.sqrt(jnp.sqrt(jnp.sqrt(jnp.abs(p))))
+    return jnp.where(p < 0.0, -v, v)
+
+
 def kernel(
     tok_ref, cot_ref, w_ref, first_ref, second_ref, slab_ref, outer_ref, mom_ref,
     proj_out, neww_out, first_out, second_out, outer_out, mom_out, local_out,
-    xb, xo, cb, co, wb, g, r1, ru, ra, m1, m2,
-    slab, ra0, ra1, pa0, pa1, rb0, rb1, tb, rz, po, pm, agb, nl,
-    acc, pj, nw,
-    ss, rs, ls, xs, slab_s, os,
+    xb, xo, cb, co, wb, g, sb, r1, ru, ra, m1, m2,
+    slab, ra0, ra1, pa0, pa1, rb0, rb1, tb, rz, po, pm, agb, acc,
+    ss, rs, ls, xs, slab_s,
 ):
     r = lax.axis_index("replica")
     f = lax.axis_index("fsdp")
@@ -143,14 +156,36 @@
         other = lax.dot_general(xo[d], co[...], dims, preferred_element_type=F32)
         g[d] += other
 
+    def pack(slot, d, lo):
+        def one(i, _):
+            at = pl.multiple_of(i * 32, 32)
+            sb[slot, pl.ds(at, 32)] = packed(g[d, pl.ds(lo + at, 32)])
+            return 0
+        lax.fori_loop(0, HB // 32, one, 0)
+
+    def join(ref, half, d, lo, slot=None):
+        def one(i, _):
+            at = pl.multiple_of(i * 32, 32)
+            total = g[d, pl.ds(lo + at, 32)] + unpacked(ref[half, pl.ds(at, 32)])
+            if slot is None:
+                g[d, pl.ds(lo + at, 32)] = total
+            else:
+                sb[slot, pl.ds(at, 32)] = packed(total)
+            return 0
+        lax.fori_loop(0, HB // 32, one, 0)
+
     c_core.wait_recv()
     gradient(2)
-    g_up1 = send(G_UP1, g.at[2, 0:HB], r1.at[0], up)
-    g_down1 = send(G_DOWN1, g.at[2, HB:B], r1.at[1], down)
+    pack(0, 2, 0)
+    g_up1 = send(G_UP1, sb.at[0], r1.at[0], up)
+    pack(1, 2, HB)
+    g_down1 = send(G_DOWN1, sb.at[1], r1.at[1], down)
     gradient(1)
-    g_up = send(G_UP, g.at[1, HB:B], ru.at[0], up)
+    pack(2, 1, HB)
+    g_up = send(G_UP, sb.at[2], ru.at[0], up)
     gradient(3)
-    g_down = send(G_DOWN, g.at[3, 0:HB], ru.at[1], down)
+    pack(3, 3, 0)
+    g_down = send(G_DOWN, sb.at[3], ru.at[1], down)
     gradient(0)
 
     def project(k, start=False):
@@ -207,25 +242,17 @@
     pseudo_grad = po[...] - average
     new_momentum = OUTER_MOMENTUM * pm[...] + pseudo_grad
     new_outer = po[...] - OUTER_RATE * (pseudo_grad + OUTER_MOMENTUM * new_momentum)
-    pm[...] = new_momentum
+    mom_out[...] = new_momentum
+    outer_out[...] = new_outer
     agb[2 * x + zl, y] = new_outer
-    outs = []
-
-    def put(place, src, dst):
-        copy = pltpu.make_async_copy(src, dst, os.at[place])
-        copy.start()
-        outs.append(copy)
-
     z_gather = send(AG_Z, agb.at[2 * x + zl, y], agb.at[2 * x + zl, y], pair)
-    put(0, pm, mom_out)
-    put(1, agb.at[2 * x + zl, y], outer_out)
 
     g_up1.wait_recv()
-    g[1, 0:HB] += r1[0]
-    g_up2 = send(G_UP2, g.at[1, 0:HB], ra.at[0], up)
+    join(r1, 0, 1, 0, 4)
+    g_up2 = send(G_UP2, sb.at[4], ra.at[0], up)
     g_down1.wait_recv()
-    g[3, HB:B] += r1[1]
-    g_down2 = send(G_DOWN2, g.at[3, HB:B], ra.at[1], down)
+    join(r1, 1, 3, HB, 5)
+    g_down2 = send(G_DOWN2, sb.at[5], ra.at[1], down)
 
     z_gather.wait_recv()
     g0 = [send(AG_A0 + d - 1, agb.at[pl.ds(2 * x, 2), y, 0:HR], agb.at[pl.ds(2 * x, 2), y, 0:HR], at_x(d)) for d in (1, 2, 3)]
@@ -243,9 +270,9 @@
     h1 = [send(AG_B1 + d - 1, agb.at[pl.ds(2 * x, 2), :, HR:ROWS], agb.at[pl.ds(2 * x, 2), :, HR:ROWS], at_x(d)) for d in (1, 2, 3)]
 
     g_up.wait_recv()
-    g[0, HB:B] += ru[0]
+    join(ru, 0, 0, HB)
     g_down.wait_recv()
-    g[0, 0:HB] += ru[1]
+    join(ru, 1, 0, 0)
 
     for copy in h0:
         copy.wait_recv()
@@ -253,8 +280,7 @@
         copy.wait_recv()
     for k in range(32):
         block = MERGE_WEIGHT * slab[k // 4, k % 4].astype(F32) + (1.0 - MERGE_WEIGHT) * agb[k // 4, k % 4]
-        nl[:, k * LANES:(k + 1) * LANES] = block.astype(BF16)
-    put(2, nl, local_out)
+        local_out[:, k * LANES:(k + 1) * LANES] = block.astype(BF16)
 
     far = 2 * turn(zh, 2) + c
     w_up2.wait_recv()
@@ -265,22 +291,21 @@
     w_far.wait_recv()
     w_far2.wait_recv()
     project(2 * turn(zh, 2) + 1 - c)
-    pj[...] = acc[...].astype(BF16)
-    put(3, pj, proj_out)
+    proj_out[...] = acc[...].astype(BF16)
 
     own_m1.wait()
     own_m2.wait()
 
     def adam(part, half):
         def body(at):
-            grad = g[0, at] + ra[half, pl.ds(at.start - half * HB, at.size)]
+            grad = g[0, at] + unpacked(ra[half, pl.ds(at.start - half * HB, at.size)])
             new_first = BETA_ONE * m1[at] + (1.0 - BETA_ONE) * grad
             new_second = BETA_TWO * m2[at] + (1.0 - BETA_TWO) * grad * grad
             weight = wb[f, at].astype(F32)
             update = new_first / FIRST_FIX / (jnp.sqrt(new_second / SECOND_FIX) + EPSILON) + DECAY_RATE * weight
-            m1[at] = new_first
-            m2[at] = new_second
-            nw[at] = (weight - INNER_RATE * update).astype(BF16)
+            first_out[at] = new_first
+            second_out[at] = new_second
+            neww_out[at] = (weight - INNER_RATE * update).astype(BF16)
 
         def one(i, _):
             body(pl.ds(pl.multiple_of(half * HB + i * 32, 32), 32))
@@ -291,13 +316,8 @@
     adam(g_up2, 0)
     g_down2.wait_recv()
     adam(g_down2, 1)
-    put(4, m1, first_out)
-    put(5, m2, second_out)
-    put(6, nw, neww_out)
     for copy in sent:
         copy.wait_send()
-    for copy in outs:
-        copy.wait()
 
 
 def shards(tokens, key_cotangent, key_weight, first_moment, second_moment, local_slab, outer_params, outer_momentum):
@@ -311,11 +331,11 @@
         jax.ShapeDtypeStruct((ROWS, 4096), BF16),
     )
     vmem = pltpu.VMEM
-    return pl.pallas_call(
+    results = pl.pallas_call(
         kernel,
-        out_shape=out_shape,
+        out_shape=tuple(pltpu.VMEM(o.shape, o.dtype) for o in out_shape),
         in_specs=[pl.BlockSpec(memory_space=pl.ANY)] * 8,
-        out_specs=(pl.BlockSpec(memory_space=pl.ANY),) * 7,
+        out_specs=(pl.BlockSpec(memory_space=pltpu.VMEM),) * 7,
         scratch_shapes=[
             vmem((8, B, B), BF16),
             vmem((4, B, B), BF16),
@@ -323,9 +343,10 @@
             vmem((B, B), BF16),
             vmem((8, B, B), BF16),
             vmem((4, B, B), F32),
-            vmem((2, HB, B), F32),
-            vmem((2, HB, B), F32),
-            vmem((2, HB, B), F32),
+            vmem((6, HB, B), BF16),
+            vmem((2, HB, B), BF16),
+            vmem((2, HB, B), BF16),
+            vmem((2, HB, B), BF16),
             vmem((B, B), F32),
             vmem((B, B), F32),
             vmem((8, 4, ROWS, LANES), BF16),
@@ -340,22 +361,35 @@
             vmem((ROWS, LANES), F32),
             vmem((ROWS, LANES), F32),
             vmem((8, 4, ROWS, LANES), F32),
-            vmem((ROWS, 4096), BF16),
             vmem((B, B), F32),
-            vmem((B, B), BF16),
-            vmem((B, B), BF16),
             pltpu.SemaphoreType.DMA((N_REMOTE,)),
             pltpu.SemaphoreType.DMA((N_REMOTE,)),
             pltpu.SemaphoreType.DMA((6,)),
             pltpu.SemaphoreType.DMA((8,)),
             pltpu.SemaphoreType.DMA((32,)),
-            pltpu.SemaphoreType.DMA((7,)),
         ],
         name="window",
         compiler_params=pltpu.CompilerParams(
-            collective_id=0, has_side_effects=True, vmem_limit_bytes=48 << 20
+            collective_id=0, has_side_effects=True, vmem_limit_bytes=40 << 20
         ),
-    )(tokens, key_cotangent, key_weight, first_moment, second_moment, local_slab, outer_params, outer_momentum)
+    )(*[pltpu.with_memory_space_constraint(a, pltpu.HBM) for a in (tokens, key_cotangent, key_weight, first_moment, second_moment, local_slab, outer_params, outer_momentum)])
+
+    def deliver(*refs):
+        copies = [pltpu.make_async_copy(refs[i], refs[7 + i], refs[14].at[i]) for i in range(7)]
+        for copy in copies:
+            copy.start()
+        for copy in copies:
+            copy.wait()
+
+    return pl.pallas_call(
+        deliver,
+        out_shape=out_shape,
+        in_specs=[pl.BlockSpec(memory_space=pltpu.VMEM)] * 7,
+        out_specs=(pl.BlockSpec(memory_space=pl.ANY),) * 7,
+        scratch_shapes=[pltpu.SemaphoreType.DMA((7,))],
+        name="deliver",
+        compiler_params=pltpu.CompilerParams(vmem_limit_bytes=8 << 20),
+    )(*results)
 
 
 def solution(mesh):

time: 147 us -> 111 us (0.76)
  Pallas kernels: 135 us -> 110 us
  local copies, waits for them, and re-layouts: 11 us -> 0 us
    pallas_call x1 -> x2, Pallas kernels: 135 us -> 110 us  [the longest x1 108 us: shards(): pl.pallas_call(kernel, out_shape=tuple((pltpu.VMEM(o.shape, o.dtype) for...]
    unnamed x19 -> x0, local copies, waits for them, and re-layouts: 11 us -> none
where the time goes in v2:
time: 111 us
  Pallas kernels  110 us (99%)
    pallas_call x1, Pallas kernels, shards(): pl.pallas_call(kernel, out_shape=tuple((pltpu.VMEM(o.shape, o.dtype) for...  108 us
    pallas_call x1, Pallas kernels, shards(): pl.pallas_call(deliver, out_shape=out_shape, in_specs=[pl.BlockSpec(memor...  2.31 us

profile of v2, /device:TPU:1, one launch (start us, length us, event | category | flops | bytes accessed | tf_op | source)
XLA Modules:
  0.0 110.9 jit_solution(15404813591342049794)
XLA Ops:
  0.6 108.0 %window.1 = (bf16[512,512]{1,0:T(8,128)(2,1)S(1)}, bf16[512,512]{1,0:T(8,128)(2,1)S(1)}, f32[512,512]{1,0:T(8,128)S(1)}, f32[512,512]{1,0:T(8,128)S(1)}, f32[192...) custom-call(bf16[512,4096]{1,0:T(8,128)(2,1)} %tok_ref.1, bf16[512,512]{1,0:T(8,128)(2,1)} %cot_ref.1, ...), custom_call_target="tpu_custom_call" | custom-call | tf_op jit(solution)/shard_map/window/pallas_call | solution.py:334
  108.6 2.3 %deliver.1 = (bf16[512,512]{1,0:T(8,128)(2,1)}, bf16[512,512]{1,0:T(8,128)(2,1)}, f32[512,512]{1,0:T(8,128)}, f32[512,512]{1,0:T(8,128)}, f32[192,128]{1,0:T(8,1...) custom-call(bf16[512,512]{1,0:T(8,128)(2,1)S(1)} %get-tuple-element.14.refs_0_, ...), custom_call_target="tpu_custom_call" | custom-call | tf_op jit(solution)/shard_map/deliver/pallas_call | solution.py:384

commit v3 on v2

v3 whole, which is shorter than its diff:
```python
import jax
import jax.numpy as jnp
from jax import lax
from jax.experimental import pallas as pl
from jax.experimental.pallas import tpu as pltpu
from jax.sharding import PartitionSpec as P

BETA_ONE = 0.9
BETA_TWO = 0.95
INNER_RATE = 0.001
DECAY_RATE = 0.1
EPSILON = 1e-08
FIRST_FIX = 1.0 - (0.9**50) ** 2
SECOND_FIX = 1.0 - (0.95**50) ** 2
OUTER_RATE = 0.7
OUTER_MOMENTUM = 0.9
MERGE_WEIGHT = 0.5

MESH = pl.DeviceIdType.MESH
F32, BF16 = jnp.float32, jnp.bfloat16
B = 512
HB = 256
ROWS = 192
HR = 96
LANES = 128
REPLICAS = 32

NZ = 1

W_CORE, W_UP2, W_DOWN2, W_CORE_UP, W_CORE_DOWN, W_CORE_FAR, W_CORE_FAR2 = range(7)
C_CORE = 9
X_CORE = 10
G_UP1, G_DOWN1, G_UP, G_DOWN, G_UP2, G_DOWN2 = range(14, 20)
S_FIRST = 20
RS_A0, RS_A1, RS_B0, RS_B1 = 26, 29, 32, 35
AG_A0, AG_A1, AG_B0, AG_B1 = 38, 41, 44, 47
RS_Z = 50
AG_Z = RS_Z + NZ
W_UP = AG_Z + NZ
W_DOWN = W_UP + 4
N_REMOTE = W_DOWN + 4


TOP = 2.0**7.75


def packed(t):
    t2 = t * t
    t4 = t2 * t2
    t8 = t4 * t4
    t16 = t8 * t8
    return jnp.where(t < 0.0, -t16, t16).astype(BF16)


def unpacked(p):
    p = p.astype(F32)
    t = jnp.sqrt(jnp.sqrt(jnp.sqrt(jnp.sqrt(jnp.abs(p)))))
    return jnp.where(p < 0.0, -t, t)


def kernel(
    tok_ref, cot_ref, w_ref, first_ref, second_ref, slab_ref, outer_ref, mom_ref,
    proj_out, neww_out, first_out, second_out, outer_out, mom_out, local_out,
    xb, xo, cb, co, wb, g, sb, sc, tiles, rg, rc, m1, m2,
    slab, ra0, ra1, pa0, pa1, rb0, rb1, tb, rz, po, pm, agb, acc,
    ss, rs, ls, xs, slab_s,
):
    r = lax.axis_index("replica")
    f = lax.axis_index("fsdp")
    x, zl, y = lax.div(r, 8), lax.rem(lax.div(r, 4), 2), lax.rem(r, 4)
    zh, c = lax.div(f, 2), lax.rem(f, 2)

    def turn(value, step, size=4):
        return lax.rem(value + step + size, size)

    def dev(x_, zl_, y_, zh_, c_):
        return {"replica": (x_ * 2 + zl_) * 4 + y_, "fsdp": zh_ * 2 + c_}

    def at_x(d):
        return dev(turn(x, d), zl, y, zh, c)

    def at_y(d):
        return dev(x, zl, turn(y, d), zh, c)

    up, down = dev(x, zl, y, turn(zh, 1), c), dev(x, zl, y, turn(zh, -1), c)
    pair = dev(x, 1 - zl, y, zh, c)
    core = dev(x, zl, y, zh, 1 - c)

    def remote(place, src, dst, device):
        return pltpu.make_async_remote_copy(
            src_ref=src, dst_ref=dst, send_sem=ss.at[place], recv_sem=rs.at[place],
            device_id=device, device_id_type=MESH,
        )

    sent = []

    def send(place, src, dst, device):
        copy = remote(place, src, dst, device)
        copy.start()
        sent.append(copy)
        return copy

    own_w = pltpu.make_async_copy(w_ref, wb.at[f], ls.at[0])
    own_w.start()
    own_c = pltpu.make_async_copy(cot_ref, cb, ls.at[1])
    own_c.start()
    own_x = []
    for k in range(8):
        copy = pltpu.make_async_copy(tok_ref.at[:, k * B:(k + 1) * B], xb.at[k], xs.at[k])
        copy.start()
        own_x.append(copy)

    def slab_copy(k):
        return pltpu.make_async_copy(
            slab_ref.at[:, k * LANES:(k + 1) * LANES], slab.at[k // 4, k % 4], slab_s.at[k]
        )
    for k in range(32):
        slab_copy(k).start()
    own_m1 = pltpu.make_async_copy(first_ref, m1, ls.at[2])
    own_m2 = pltpu.make_async_copy(second_ref, m2, ls.at[3])
    own_po = pltpu.make_async_copy(outer_ref, po, ls.at[4])
    own_pm = pltpu.make_async_copy(mom_ref, pm, ls.at[5])
    for copy in (own_po, own_pm, own_m1, own_m2):
        copy.start()

    barrier = pltpu.get_barrier_semaphore()
    partners = [up, down, core, pair] + [at_x(d) for d in (1, 2, 3)] + [at_y(d) for d in (1, 2, 3)]
    for partner in partners:
        pl.semaphore_signal(barrier, inc=1, device_id=partner, device_id_type=MESH)
    pl.semaphore_wait(barrier, len(partners))

    copies = {}

    def arrived(*names):
        for name in names:
            copies[name].wait_recv()

    def send_w(*parts):
        for i in parts:
            for name, place, device, at in (("w_up", W_UP, up, i), ("w_down", W_DOWN, down, 3 - i)):
                part = wb.at[f, at * 128:(at + 1) * 128]
                copies[name, i] = send(place + i, part, part, device)

    def send_core():
        own_c.wait()
        copies["c_core"] = send(C_CORE, cb, co, core)
        for copy in own_x:
            copy.wait()
        for d in (2, 1, 3, 0):
            copies["x_core", d] = send(X_CORE + d, xb.at[2 * turn(zh, d) + 1 - c], xo.at[d], core)

    def send_w_core():
        copies["w_core"] = send(W_CORE, wb.at[f], wb.at[f], core)

    def frag_send():
        for k in range(32):
            slab_copy(k).wait()
        for d in (1, 2, 3):
            copies["a0", d] = send(RS_A0 + d - 1, slab.at[pl.ds(2 * turn(x, d), 2), :, 0:HR], ra0.at[d - 1], at_x(d))
            copies["a1", d] = send(RS_A1 + d - 1, slab.at[:, turn(y, d), HR:ROWS], ra1.at[d - 1], at_y(d))

    def gradient(d):
        arrived(("x_core", d))
        dims = (((0,), (0,)), ((), ()))
        g[d] = lax.dot_general(xb[2 * turn(zh, d) + c], cb[...], dims, preferred_element_type=F32)
        g[d] += lax.dot_general(xo[d], co[...], dims, preferred_element_type=F32)

    def chunks(body):
        def one(i, _):
            body(pl.multiple_of(i * 32, 32))
            return 0
        lax.fori_loop(0, HB // 32, one, 0)

    def spread(tile):
        wide = jnp.concatenate([tile] * 4, axis=1)
        return jnp.concatenate([wide] * 4, axis=0)

    def scale_tile(slot, d, lo):
        tiles[0] = jnp.zeros((32, B), F32)

        def body(at):
            tiles[0] = jnp.maximum(tiles[0], jnp.abs(g[d, pl.ds(lo + at, 32)]))
        chunks(body)
        top = tiles[0]
        top = jnp.maximum(jnp.maximum(top[0:8], top[8:16]), jnp.maximum(top[16:24], top[24:32]))
        top = jnp.maximum(jnp.maximum(top[:, 0:128], top[:, 128:256]), jnp.maximum(top[:, 256:384], top[:, 384:512]))
        top = jnp.maximum(top, 1e-30)
        sc[slot] = top
        tiles[0] = spread(TOP / top)

    def pack(slot, d, lo):
        scale_tile(slot, d, lo)

        def body(at):
            sb[slot, pl.ds(at, 32)] = packed(g[d, pl.ds(lo + at, 32)] * tiles[0])
        chunks(body)

    def join(half, d, lo):
        tiles[1] = spread(rc[half] * (1.0 / TOP))

        def body(at):
            g[d, pl.ds(lo + at, 32)] += unpacked(rg[half, pl.ds(at, 32)]) * tiles[1]
        chunks(body)

    def send_g(name, place, slot, device):
        copies[name] = send(place, sb.at[slot], rg.at[slot], device)
        copies[name + "s"] = send(S_FIRST + slot, sc.at[slot], rc.at[slot], device)

    def arrived_g(*names):
        for name in names:
            arrived(name, name + "s")

    def grad_first():
        arrived("c_core")
        gradient(2)
        pack(0, 2, 0)
        send_g("g_up1", G_UP1, 0, up)
        pack(1, 2, HB)
        send_g("g_down1", G_DOWN1, 1, down)

    def grad_near():
        gradient(1)
        pack(2, 1, HB)
        gradient(3)
        pack(3, 3, 0)

    def send_near():
        send_g("g_up", G_UP, 2, up)
        send_g("g_down", G_DOWN, 3, down)

    def grad_join():
        arrived_g("g_up1")
        join(0, 1, 0)
        pack(4, 1, 0)
        send_g("g_up2", G_UP2, 4, up)
        arrived_g("g_down1")
        join(1, 3, HB)
        pack(5, 3, HB)
        send_g("g_down2", G_DOWN2, 5, down)

    def grad_fold():
        arrived_g("g_up")
        join(2, 0, HB)
        arrived_g("g_down")
        join(3, 0, 0)

    def project(k, start=False):
        part = jnp.dot(xb[k], wb[k], preferred_element_type=F32)
        if start:
            acc[...] = part
        else:
            acc[...] += part

    def project_core():
        arrived("w_core")
        project(2 * zh + 1 - c)

    def frag_a():
        arrived(("a0", 1), ("a0", 2), ("a0", 3))
        for kk in range(2):
            for yy in range(4):
                pa0[kk, yy] = (
                    slab[2 * x + kk, yy, 0:HR].astype(F32) + ra0[0, kk, yy].astype(F32)
                    + ra0[1, kk, yy].astype(F32) + ra0[2, kk, yy].astype(F32)
                )
        for d in (1, 2, 3):
            copies["b0", d] = send(RS_B0 + d - 1, pa0.at[:, turn(y, d)], rb0.at[d - 1], at_y(d))
        arrived(("a1", 1), ("a1", 2), ("a1", 3))
        for k in range(8):
            pa1[k] = (
                slab[k, y, HR:ROWS].astype(F32) + ra1[0, k].astype(F32)
                + ra1[1, k].astype(F32) + ra1[2, k].astype(F32)
            )
        for d in (1, 2, 3):
            copies["b1", d] = send(RS_B1 + d - 1, pa1.at[pl.ds(2 * turn(x, d), 2)], rb1.at[d - 1], at_x(d))

    def frag_b():
        for d in (1, 2, 3):
            arrived(("b0", d), ("b1", d))
        for kk in range(2):
            tb[kk, 0:HR] = pa0[kk, y] + rb0[0, kk] + rb0[1, kk] + rb0[2, kk]
            tb[kk, HR:ROWS] = pa1[2 * x + kk] + rb1[0, kk] + rb1[1, kk] + rb1[2, kk]
        for i in range(NZ):
            part = pl.ds(i * (ROWS // NZ), ROWS // NZ)
            copies["z_sum", i] = send(RS_Z + i, tb.at[1 - zl, part], rz.at[part], pair)

    below, above, far = 2 * turn(zh, -1) + c, 2 * turn(zh, 1) + c, 2 * turn(zh, 2) + c

    def w_on():
        arrived(("w_up", 0), ("w_up", 1))
        copies["w_up2"] = send(W_UP2, wb.at[below, 0:HB], wb.at[below, 0:HB], up)
        arrived(("w_down", 0), ("w_down", 1))
        copies["w_down2"] = send(W_DOWN2, wb.at[above, HB:B], wb.at[above, HB:B], down)

    def w_share():
        arrived(("w_up", 2), ("w_up", 3))
        copies["w_core_up"] = send(W_CORE_UP, wb.at[below], wb.at[below], core)
        arrived(("w_down", 2), ("w_down", 3))
        copies["w_core_down"] = send(W_CORE_DOWN, wb.at[above], wb.at[above], core)

    def frag_update():
        arrived(*[("z_sum", i) for i in range(NZ)])
        own_po.wait()
        own_pm.wait()
        average = (tb[zl] + rz[...]) / REPLICAS
        pseudo_grad = po[...] - average
        new_momentum = OUTER_MOMENTUM * pm[...] + pseudo_grad
        new_outer = po[...] - OUTER_RATE * (pseudo_grad + OUTER_MOMENTUM * new_momentum)
        mom_out[...] = new_momentum
        outer_out[...] = new_outer
        agb[2 * x + zl, y] = new_outer
        for i in range(NZ):
            part = agb.at[2 * x + zl, y, pl.ds(i * (ROWS // NZ), ROWS // NZ)]
            copies["z_gather", i] = send(AG_Z + i, part, part, pair)

    def frag_c():
        arrived(*[("z_gather", i) for i in range(NZ)])
        for d in (1, 2, 3):
            lower, upper = agb.at[pl.ds(2 * x, 2), y, 0:HR], agb.at[pl.ds(2 * x, 2), y, HR:ROWS]
            copies["c0", d] = send(AG_A0 + d - 1, lower, lower, at_x(d))
            copies["c1", d] = send(AG_A1 + d - 1, upper, upper, at_y(d))

    def frag_d():
        arrived(("c0", 1), ("c0", 2), ("c0", 3))
        for d in (1, 2, 3):
            lower = agb.at[:, y, 0:HR]
            copies["d0", d] = send(AG_B0 + d - 1, lower, lower, at_y(d))
        arrived(("c1", 1), ("c1", 2), ("c1", 3))
        for d in (1, 2, 3):
            upper = agb.at[pl.ds(2 * x, 2), :, HR:ROWS]
            copies["d1", d] = send(AG_B1 + d - 1, upper, upper, at_x(d))

    def frag_merge():
        for d in (1, 2, 3):
            arrived(("d0", d), ("d1", d))
        for k in range(32):
            block = MERGE_WEIGHT * slab[k // 4, k % 4].astype(F32) + (1.0 - MERGE_WEIGHT) * agb[k // 4, k % 4]
            local_out[:, k * LANES:(k + 1) * LANES] = block.astype(BF16)

    def project_near():
        arrived("w_core_up", "w_core_down")
        for s in (-1, 1):
            project(2 * turn(zh, s) + c)
            project(2 * turn(zh, s) + 1 - c)

    def w_far():
        arrived("w_up2")
        copies["w_far"] = send(W_CORE_FAR, wb.at[far, 0:HB], wb.at[far, 0:HB], core)
        arrived("w_down2")
        copies["w_far2"] = send(W_CORE_FAR2, wb.at[far, HB:B], wb.at[far, HB:B], core)

    def project_far():
        project(far)
        arrived("w_far", "w_far2")
        project(2 * turn(zh, 2) + 1 - c)
        proj_out[...] = acc[...].astype(BF16)

    def adam(half):
        tiles[1] = spread(rc[4 + half] * (1.0 / TOP))

        def body(at):
            rows_at = pl.ds(half * HB + at, 32)
            grad = g[0, rows_at] + unpacked(rg[4 + half, pl.ds(at, 32)]) * tiles[1]
            new_first = BETA_ONE * m1[rows_at] + (1.0 - BETA_ONE) * grad
            new_second = BETA_TWO * m2[rows_at] + (1.0 - BETA_TWO) * grad * grad
            weight = wb[f, rows_at].astype(F32)
            update = new_first / FIRST_FIX / (jnp.sqrt(new_second / SECOND_FIX) + EPSILON) + DECAY_RATE * weight
            first_out[rows_at] = new_first
            second_out[rows_at] = new_second
            neww_out[rows_at] = (weight - INNER_RATE * update).astype(BF16)
        chunks(body)

    def inner():
        own_m1.wait()
        own_m2.wait()
        arrived_g("g_up2")
        adam(0)
        arrived_g("g_down2")
        adam(1)

    own_w.wait()
    send_w(0, 1)
    send_core()
    send_w_core()
    frag_send()
    grad_first()
    grad_near()
    gradient(0)
    project(f, True)
    frag_a()
    project_core()
    frag_b()
    send_w(2)
    frag_update()
    send_w(3)
    grad_join()
    frag_c()
    send_near()
    w_on()
    w_share()
    project_near()
    frag_d()
    grad_fold()
    frag_merge()
    inner()
    w_far()
    project_far()
    for copy in sent:
        copy.wait_send()


def shards(tokens, key_cotangent, key_weight, first_moment, second_moment, local_slab, outer_params, outer_momentum):
    out_shape = (
        jax.ShapeDtypeStruct((B, B), BF16),
        jax.ShapeDtypeStruct((B, B), BF16),
        jax.ShapeDtypeStruct((B, B), F32),
        jax.ShapeDtypeStruct((B, B), F32),
        jax.ShapeDtypeStruct((ROWS, LANES), F32),
        jax.ShapeDtypeStruct((ROWS, LANES), F32),
        jax.ShapeDtypeStruct((ROWS, 4096), BF16),
    )
    vmem = pltpu.VMEM
    results = pl.pallas_call(
        kernel,
        out_shape=tuple(pltpu.VMEM(o.shape, o.dtype) for o in out_shape),
        in_specs=[pl.BlockSpec(memory_space=pl.ANY)] * 8,
        out_specs=(pl.BlockSpec(memory_space=pltpu.VMEM),) * 7,
        scratch_shapes=[
            vmem((8, B, B), BF16),
            vmem((4, B, B), BF16),
            vmem((B, B), BF16),
            vmem((B, B), BF16),
            vmem((8, B, B), BF16),
            vmem((4, B, B), F32),
            vmem((6, HB, B), BF16),
            vmem((6, 8, LANES), F32),
            vmem((2, 32, B), F32),
            vmem((6, HB, B), BF16),
            vmem((6, 8, LANES), F32),
            vmem((B, B), F32),
            vmem((B, B), F32),
            vmem((8, 4, ROWS, LANES), BF16),
            vmem((3, 2, 4, HR, LANES), BF16),
            vmem((3, 8, HR, LANES), BF16),
            vmem((2, 4, HR, LANES), F32),
            vmem((8, HR, LANES), F32),
            vmem((3, 2, HR, LANES), F32),
            vmem((3, 2, HR, LANES), F32),
            vmem((2, ROWS, LANES), F32),
            vmem((ROWS, LANES), F32),
            vmem((ROWS, LANES), F32),
            vmem((ROWS, LANES), F32),
            vmem((8, 4, ROWS, LANES), F32),
            vmem((B, B), F32),
            pltpu.SemaphoreType.DMA((N_REMOTE,)),
            pltpu.SemaphoreType.DMA((N_REMOTE,)),
            pltpu.SemaphoreType.DMA((6,)),
            pltpu.SemaphoreType.DMA((8,)),
            pltpu.SemaphoreType.DMA((32,)),
        ],
        name="window",
        compiler_params=pltpu.CompilerParams(
            collective_id=0, has_side_effects=True, vmem_limit_bytes=40 << 20
        ),
    )(*[pltpu.with_memory_space_constraint(a, pltpu.HBM) for a in (tokens, key_cotangent, key_weight, first_moment, second_moment, local_slab, outer_params, outer_momentum)])

    def deliver(*refs):
        copies = [pltpu.make_async_copy(refs[i], refs[7 + i], refs[14].at[i]) for i in range(7)]
        for copy in copies:
            copy.start()
        for copy in copies:
            copy.wait()

    return pl.pallas_call(
        deliver,
        out_shape=out_shape,
        in_specs=[pl.BlockSpec(memory_space=pltpu.VMEM)] * 7,
        out_specs=(pl.BlockSpec(memory_space=pl.ANY),) * 7,
        scratch_shapes=[pltpu.SemaphoreType.DMA((7,))],
        name="deliver",
        compiler_params=pltpu.CompilerParams(vmem_limit_bytes=8 << 20),
    )(*results)


def solution(mesh):
    both = P(("replica", "fsdp"), None)
    cut = P("fsdp", "replica")
    return jax.shard_map(
        shards,
        mesh=mesh,
        in_specs=(both, both, both, both, both, both, cut, cut),
        out_specs=(both, both, both, both, cut, cut, both),
        check_vma=False,
    )
```

time: 111 us -> 92.6 us (0.83)
  Pallas kernels: 110 us -> 91.5 us
    pallas_call x1, Pallas kernels: 108 us -> 89.2 us  [shards(): pl.pallas_call(kernel, out_shape=tuple((pltpu.VMEM(o.shape, o.dtype) for...]
where the time goes in v3:
time: 92.6 us; the launch traced here: 92.2 us
  Pallas kernels  91.5 us (99%)
    pallas_call x1, Pallas kernels, shards(): pl.pallas_call(kernel, out_shape=tuple((pltpu.VMEM(o.shape, o.dtype) for...  89.2 us
    pallas_call x1, Pallas kernels, shards(): pl.pallas_call(deliver, out_shape=out_shape, in_specs=[pl.BlockSpec(memor...  2.31 us

profile of v3, /device:TPU:1, one launch (start us, length us, event | category | flops | bytes accessed | tf_op | source)
XLA Modules:
  0.0 92.2 jit_solution(136525480550423498)
XLA Ops:
  0.6 89.2 %window.1 = (bf16[512,512]{1,0:T(8,128)(2,1)S(1)}, bf16[512,512]{1,0:T(8,128)(2,1)S(1)}, f32[512,512]{1,0:T(8,128)S(1)}, f32[512,512]{1,0:T(8,128)S(1)}, f32[192...) custom-call(bf16[512,4096]{1,0:T(8,128)(2,1)} %tok_ref.1, bf16[512,512]{1,0:T(8,128)(2,1)} %cot_ref.1, ...), custom_call_target="tpu_custom_call" | custom-call | tf_op jit(solution)/shard_map/window/pallas_call | solution.py:423
  89.9 2.3 %deliver.1 = (bf16[512,512]{1,0:T(8,128)(2,1)}, bf16[512,512]{1,0:T(8,128)(2,1)}, f32[512,512]{1,0:T(8,128)}, f32[512,512]{1,0:T(8,128)}, f32[192,128]{1,0:T(8,1...) custom-call(bf16[512,512]{1,0:T(8,128)(2,1)S(1)} %get-tuple-element.14.refs_0_, ...), custom_call_target="tpu_custom_call" | custom-call | tf_op jit(solution)/shard_map/deliver/pallas_call | solution.py:474

commit v4 on v3

--- a/solution.py
+++ b/solution.py
@@ -100,6 +100,11 @@
         sent.append(copy)
         return copy
 
+    barrier = pltpu.get_barrier_semaphore()
+    partners = [up, down, core, pair] + [at_x(d) for d in (1, 2, 3)] + [at_y(d) for d in (1, 2, 3)]
+    for partner in partners:
+        pl.semaphore_signal(barrier, inc=1, device_id=partner, device_id_type=MESH)
+
     own_w = pltpu.make_async_copy(w_ref, wb.at[f], ls.at[0])
     own_w.start()
     own_c = pltpu.make_async_copy(cot_ref, cb, ls.at[1])
@@ -114,8 +119,6 @@
         return pltpu.make_async_copy(
             slab_ref.at[:, k * LANES:(k + 1) * LANES], slab.at[k // 4, k % 4], slab_s.at[k]
         )
-    for k in range(32):
-        slab_copy(k).start()
     own_m1 = pltpu.make_async_copy(first_ref, m1, ls.at[2])
     own_m2 = pltpu.make_async_copy(second_ref, m2, ls.at[3])
     own_po = pltpu.make_async_copy(outer_ref, po, ls.at[4])
@@ -123,10 +126,6 @@
     for copy in (own_po, own_pm, own_m1, own_m2):
         copy.start()
 
-    barrier = pltpu.get_barrier_semaphore()
-    partners = [up, down, core, pair] + [at_x(d) for d in (1, 2, 3)] + [at_y(d) for d in (1, 2, 3)]
-    for partner in partners:
-        pl.semaphore_signal(barrier, inc=1, device_id=partner, device_id_type=MESH)
     pl.semaphore_wait(barrier, len(partners))
 
     copies = {}
@@ -140,6 +139,10 @@
             for name, place, device, at in (("w_up", W_UP, up, i), ("w_down", W_DOWN, down, 3 - i)):
                 part = wb.at[f, at * 128:(at + 1) * 128]
                 copies[name, i] = send(place + i, part, part, device)
+
+    def load_slab():
+        for k in range(32):
+            slab_copy(k).start()
 
     def send_core():
         own_c.wait()
@@ -380,6 +383,7 @@
 
     own_w.wait()
     send_w(0, 1)
+    load_slab()
     send_core()
     send_w_core()
     frag_send()
@@ -392,9 +396,9 @@
     frag_b()
     send_w(2)
     frag_update()
+    frag_c()
     send_w(3)
     grad_join()
-    frag_c()
     send_near()
     w_on()
     w_share()

time: 92.6 us -> 90.4 us (0.976)
  the two profiles are of different devices: /device:TPU:1 before, /device:TPU:33 now
where the time goes in v4:
time: 90.4 us; the launch traced here: 90.2 us
  Pallas kernels  89.6 us (99%)
    pallas_call x1, Pallas kernels, shards(): pl.pallas_call(kernel, out_shape=tuple((pltpu.VMEM(o.shape, o.dtype) for...  87.3 us
    pallas_call x1, Pallas kernels, shards(): pl.pallas_call(deliver, out_shape=out_shape, in_specs=[pl.BlockSpec(memor...  2.31 us

profile of v4, /device:TPU:33, one launch (start us, length us, event | category | flops | bytes accessed | tf_op | source)
XLA Modules:
  0.0 90.2 jit_solution(5684771673876679801)
XLA Ops:
  0.6 87.3 %window.1 = (bf16[512,512]{1,0:T(8,128)(2,1)S(1)}, bf16[512,512]{1,0:T(8,128)(2,1)S(1)}, f32[512,512]{1,0:T(8,128)S(1)}, f32[512,512]{1,0:T(8,128)S(1)}, f32[192...) custom-call(bf16[512,4096]{1,0:T(8,128)(2,1)} %tok_ref.1, bf16[512,512]{1,0:T(8,128)(2,1)} %cot_ref.1, ...), custom_call_target="tpu_custom_call" | custom-call | tf_op jit(solution)/shard_map/window/pallas_call | solution.py:427
  87.9 2.3 %deliver.1 = (bf16[512,512]{1,0:T(8,128)(2,1)}, bf16[512,512]{1,0:T(8,128)(2,1)}, f32[512,512]{1,0:T(8,128)}, f32[512,512]{1,0:T(8,128)}, f32[192,128]{1,0:T(8,1...) custom-call(bf16[512,512]{1,0:T(8,128)(2,1)S(1)} %get-tuple-element.14.refs_0_, ...), custom_call_target="tpu_custom_call" | custom-call | tf_op jit(solution)/shard_map/deliver/pallas_call | solution.py:478

commit v5 on v4

--- a/solution.py
+++ b/solution.py
@@ -385,13 +385,13 @@
     send_w(0, 1)
     load_slab()
     send_core()
+    frag_send()
     send_w_core()
-    frag_send()
     grad_first()
+    frag_a()
     grad_near()
     gradient(0)
     project(f, True)
-    frag_a()
     project_core()
     frag_b()
     send_w(2)

time: 90.4 us -> 90.4 us (level)
  the two profiles are of different devices: /device:TPU:33 before, /device:TPU:1 now
where the time goes in v5:
time: 90.4 us; the launch traced here: 89 us
  Pallas kernels  88.3 us (98%)
    pallas_call x1, Pallas kernels, shards(): pl.pallas_call(kernel, out_shape=tuple((pltpu.VMEM(o.shape, o.dtype) for...  86 us
    pallas_call x1, Pallas kernels, shards(): pl.pallas_call(deliver, out_shape=out_shape, in_specs=[pl.BlockSpec(memor...  2.31 us

profile of v5, /device:TPU:1, one launch (start us, length us, event | category | flops | bytes accessed | tf_op | source)
XLA Modules:
  0.0 89.0 jit_solution(12253132976437704859)
XLA Ops:
  0.6 86.0 %window.1 = (bf16[512,512]{1,0:T(8,128)(2,1)S(1)}, bf16[512,512]{1,0:T(8,128)(2,1)S(1)}, f32[512,512]{1,0:T(8,128)S(1)}, f32[512,512]{1,0:T(8,128)S(1)}, f32[192...) custom-call(bf16[512,4096]{1,0:T(8,128)(2,1)} %tok_ref.1, bf16[512,512]{1,0:T(8,128)(2,1)} %cot_ref.1, ...), custom_call_target="tpu_custom_call" | custom-call | tf_op jit(solution)/shard_map/window/pallas_call | solution.py:427
  86.6 2.3 %deliver.1 = (bf16[512,512]{1,0:T(8,128)(2,1)}, bf16[512,512]{1,0:T(8,128)(2,1)}, f32[512,512]{1,0:T(8,128)}, f32[512,512]{1,0:T(8,128)}, f32[192,128]{1,0:T(8,1...) custom-call(bf16[512,512]{1,0:T(8,128)(2,1)S(1)} %get-tuple-element.14.refs_0_, ...), custom_call_target="tpu_custom_call" | custom-call | tf_op jit(solution)/shard_map/deliver/pallas_call | solution.py:478
